TPU v7x, 32 devices: a whole 2x2x4 slice. The times are simulated.
32 devices in a mesh: patch: 16 (over z, y, x), rep: 2 (over core).
Axes of the slice: x: 2, y: 2, z: 4, core: 2. Of those that a mesh axis runs over, the one named last changes fastest.
Arguments:
- tokens: bfloat16 [8192, 512], P(('patch', 'rep')), may hold values from -6 to 6
- cotangent: bfloat16 [8192, 512], P(('patch', 'rep')), may hold values from -6 to 6
- dest: int32 [8192], P(('patch', 'rep')), may hold values from 0 to 15, as said below
- neighbours: int32 [8192, 16], P(('patch', 'rep')), may hold values from 0 to 8191, as said below
- w_qkv: bfloat16 [512, 1536], replicated, may hold values from -0.25 to 0.25
- w_out: bfloat16 [512, 512], replicated, may hold values from -1 to 1
- w_up: bfloat16 [512, 2048], replicated, may hold values from -0.25 to 0.25
- w_down: bfloat16 [2048, 512], replicated, may hold values from -0.125 to 0.125
- ada_attn: float32 [32, 1024], replicated, may hold values from -0.5 to 0.5
- ada_mlp: float32 [32, 1024], replicated, may hold values from -0.5 to 0.5
- cond: float32 [32], replicated, may hold values from -4 to 4
Outputs:
- output: bfloat16 [8192, 512], P(('patch', 'rep'))
- grad_tokens: bfloat16 [8192, 512], P(('patch', 'rep'))
- grad_qkv: float32 [512, 1536], replicated
- grad_out: float32 [512, 512], replicated
- grad_up: float32 [512, 2048], replicated
- grad_down: float32 [2048, 512], replicated
- grad_ada_attn: float32 [32, 1024], replicated
- grad_ada_mlp: float32 [32, 1024], replicated
- grad_cond: float32 [32], replicated
Inputs may be any that keep to these rules, and one draw needn't show every extreme that they name: `dest`: within each index of rep, every patch receives exactly 256 rows; one device sends at most 17 rows to one patch, and each device sends exactly 17 rows to some patch. neighbours[i, 0] = i; every other neighbour of a node in patch q lies in the rows of the same index of rep in patch q - 1, q or q + 1, counted cyclically over 16 patches; positions may repeat.
All inputs are finite; a program needn't handle non-finite values.
Results may differ from a plain program's by a relative error of at most 0.013.
Values may be sent and summed in bfloat16 or wider, within the bound.
A program may use at most 128 MiB of HBM per device.

v0:
```python
import jax
import jax.numpy as jnp
from jax import lax
from jax.sharding import PartitionSpec as P

H = 4
HD = 128
NEIGH = 16
NORM_EPS = 1e-05


def extended(cells, sides, width):
    for axis, dim in sides:
        count = lax.axis_size(axis)
        head = lax.slice_in_dim(cells, 0, width, axis=dim)
        tail = lax.slice_in_dim(cells, cells.shape[dim] - width, cells.shape[dim], axis=dim)
        cells = jnp.concatenate(
            [
                lax.ppermute(tail, axis, [(i, (i + 1) % count) for i in range(count)]),
                cells,
                lax.ppermute(head, axis, [((i + 1) % count, i) for i in range(count)]),
            ],
            axis=dim,
        )
    return cells


def from_behind(array, axis, by):
    size = lax.axis_size(axis)
    return lax.ppermute(array, axis, [(i, (i + by) % size) for i in range(size)])


def norm_parts(values_in):
    centre = jnp.mean(values_in, axis=-1, keepdims=True)
    centred = values_in - centre
    inverse = lax.rsqrt(jnp.mean(centred * centred, axis=-1, keepdims=True) + NORM_EPS)
    return (centred * inverse, inverse)


def norm_back(grad_normed, plain, inverse, coeffs):
    feature_width = plain.shape[-1]
    scaled = grad_normed * (1.0 + coeffs[:feature_width])
    inner = (
        scaled
        - jnp.mean(scaled, axis=-1, keepdims=True)
        - plain * jnp.mean(scaled * plain, axis=-1, keepdims=True)
    )
    coeff_grad = jnp.concatenate(
        [jnp.sum(grad_normed * plain, axis=0), jnp.sum(grad_normed, axis=0)]
    )
    return (inverse * inner, coeff_grad)


def local(tokens, cotangent, dest, neighbours, w_qkv, w_out, w_up, w_down, ada_attn, ada_mlp, cond):
    highest = lax.Precision.HIGHEST
    row_count = tokens.shape[0]
    feature_width = tokens.shape[1]
    patch_count = lax.axis_size("patch")
    group_count = lax.axis_size("rep")
    capacity = row_count // patch_count + 1
    one_hot = (dest[:, None] == jnp.arange(patch_count, dtype=jnp.int32)[None, :]).astype(jnp.int32)
    earlier = jnp.cumsum(one_hot, axis=0) - one_hot
    slot_index = jnp.sum(earlier * one_hot, axis=1)
    sent_counts = jnp.sum(one_hot, axis=0)
    flat_slot = dest * capacity + slot_index
    outgoing = jnp.zeros((patch_count * capacity, 2 * feature_width), jnp.bfloat16)
    outgoing = outgoing.at[flat_slot].set(jnp.concatenate([tokens, cotangent], axis=1))
    arrived, arrived_counts = (
        lax.all_to_all(
            outgoing.reshape(patch_count, capacity, 2 * feature_width),
            "patch",
            split_axis=0,
            concat_axis=0,
            tiled=True,
        ),
        lax.all_to_all(sent_counts[:, None], "patch", split_axis=0, concat_axis=0, tiled=True),
    )
    counts_in = arrived_counts[:, 0]
    offsets = jnp.cumsum(counts_in) - counts_in
    columns = jnp.arange(capacity, dtype=jnp.int32)
    target = jnp.where(
        columns[None, :] < counts_in[:, None], offsets[:, None] + columns[None, :], row_count
    ).reshape(-1)
    placed = (
        jnp.zeros((row_count + 1, 2 * feature_width), jnp.bfloat16)
        .at[target]
        .set(arrived.reshape(-1, 2 * feature_width))[:row_count]
    )
    node_rows = placed[:, :feature_width].astype(jnp.float32)
    upstream = placed[:, feature_width:]
    coeff_attn = jnp.dot(cond, ada_attn, precision=highest)
    coeff_mlp = jnp.dot(cond, ada_mlp, precision=highest)
    plain_first, inv_first = norm_parts(node_rows)
    normed = (plain_first * (1.0 + coeff_attn[:feature_width]) + coeff_attn[feature_width:]).astype(
        jnp.bfloat16
    )
    projected = jnp.dot(normed, w_qkv, preferred_element_type=jnp.float32)
    queries = projected[:, :feature_width].astype(jnp.bfloat16)
    key_value = projected[:, feature_width:].astype(jnp.bfloat16)
    beside_all = extended(normed, (("patch", 0),), row_count)
    side_rows = jnp.concatenate([beside_all[:row_count], beside_all[2 * row_count :]], axis=0)
    side_kv = jnp.dot(
        side_rows, w_qkv[:, feature_width:], preferred_element_type=jnp.float32
    ).astype(jnp.bfloat16)
    kv_table = jnp.concatenate([side_kv[:row_count], key_value, side_kv[row_count:]], axis=0)
    my_patch = lax.axis_index("patch")
    owners = neighbours // row_count // group_count
    local_row = neighbours % row_count
    rel_patch = (owners - my_patch) % patch_count
    table_index = jnp.where(
        rel_patch == 0,
        row_count + local_row,
        jnp.where(rel_patch == 1, 2 * row_count + local_row, local_row),
    )
    block_rows = min(512, row_count)
    block_count = row_count // block_rows
    score_scale = 1.0 / HD**0.5

    def gather_block(index_block):
        gathered = kv_table[index_block]
        key_block = gathered[..., :feature_width].reshape(block_rows, NEIGH, H, HD)
        value_block = gathered[..., feature_width:].reshape(block_rows, NEIGH, H, HD)
        return (key_block, value_block)

    def forward_block(pieces):
        query_block, index_block = pieces
        key_block, value_block = gather_block(index_block)
        scores = (
            jnp.einsum(
                "bhd,bjhd->bhj",
                query_block.reshape(block_rows, H, HD),
                key_block,
                preferred_element_type=jnp.float32,
            )
            * score_scale
        )
        row_max = jnp.max(scores, axis=-1, keepdims=True)
        row_total = jnp.sum(jnp.exp(scores - row_max), axis=-1, keepdims=True)
        log_total = row_max + jnp.log(row_total)
        weights = jnp.exp(scores - log_total).astype(jnp.bfloat16)
        mixture = jnp.einsum(
            "bhj,bjhd->bhd", weights, value_block, preferred_element_type=jnp.float32
        )
        return (mixture.reshape(block_rows, feature_width).astype(jnp.bfloat16), log_total[..., 0])

    query_blocks = queries.reshape(block_count, block_rows, feature_width)
    index_blocks = table_index.reshape(block_count, block_rows, NEIGH)
    heads_out, log_totals = lax.map(forward_block, (query_blocks, index_blocks))
    heads_out = heads_out.reshape(row_count, feature_width)
    residual = node_rows + jnp.dot(heads_out, w_out, preferred_element_type=jnp.float32)
    plain_second, inv_second = norm_parts(residual)
    normed_mlp = (
        plain_second * (1.0 + coeff_mlp[:feature_width]) + coeff_mlp[feature_width:]
    ).astype(jnp.bfloat16)
    up_proj = jnp.dot(normed_mlp, w_up, preferred_element_type=jnp.float32)
    activation = jax.nn.silu(up_proj).astype(jnp.bfloat16)
    output_rows = residual + jnp.dot(activation, w_down, preferred_element_type=jnp.float32)
    gradient_down = jnp.einsum(
        "ri,rj->ij", activation, upstream, preferred_element_type=jnp.float32
    )
    grad_act = jnp.einsum("rj,ij->ri", upstream, w_down, preferred_element_type=jnp.float32)
    sigmoid_up = jax.nn.sigmoid(up_proj)
    grad_upproj = (grad_act * sigmoid_up * (1.0 + up_proj * (1.0 - sigmoid_up))).astype(
        jnp.bfloat16
    )
    gradient_up = jnp.einsum(
        "ri,rj->ij", normed_mlp, grad_upproj, preferred_element_type=jnp.float32
    )
    grad_normed_mlp = jnp.einsum("rj,ij->ri", grad_upproj, w_up, preferred_element_type=jnp.float32)
    grad_resid_norm, coeff_mlp_grad = norm_back(
        grad_normed_mlp, plain_second, inv_second, coeff_mlp
    )
    grad_residual = upstream.astype(jnp.float32) + grad_resid_norm
    grad_branch = grad_residual.astype(jnp.bfloat16)
    gradient_out = jnp.einsum(
        "ri,rj->ij", heads_out, grad_branch, preferred_element_type=jnp.float32
    )
    grad_heads = jnp.einsum(
        "rj,ij->ri", grad_branch, w_out, preferred_element_type=jnp.float32
    ).astype(jnp.bfloat16)

    def backward_block(table_grad, pieces):
        query_block, index_block, log_block, heads_grad = pieces
        key_block, value_block = gather_block(index_block)
        query_heads = query_block.reshape(block_rows, H, HD)
        scores = (
            jnp.einsum("bhd,bjhd->bhj", query_heads, key_block, preferred_element_type=jnp.float32)
            * score_scale
        )
        weights = jnp.exp(scores - log_block[..., None])
        weights_low = weights.astype(jnp.bfloat16)
        grad_heads_block = heads_grad.reshape(block_rows, H, HD)
        grad_weights = jnp.einsum(
            "bhd,bjhd->bhj", grad_heads_block, value_block, preferred_element_type=jnp.float32
        )
        grad_scores = weights * (
            grad_weights - jnp.sum(weights * grad_weights, axis=-1, keepdims=True)
        )
        scores_low = grad_scores.astype(jnp.bfloat16)
        grad_query = (
            jnp.einsum("bhj,bjhd->bhd", scores_low, key_block, preferred_element_type=jnp.float32)
            * score_scale
        )
        grad_key = (
            jnp.einsum("bhj,bhd->bjhd", scores_low, query_heads, preferred_element_type=jnp.float32)
            * score_scale
        )
        grad_value = jnp.einsum(
            "bhj,bhd->bjhd", weights_low, grad_heads_block, preferred_element_type=jnp.float32
        )
        pair_grad = jnp.concatenate(
            [
                grad_key.reshape(block_rows * NEIGH, feature_width),
                grad_value.reshape(block_rows * NEIGH, feature_width),
            ],
            axis=1,
        )
        table_grad = table_grad.at[index_block.reshape(-1)].add(pair_grad)
        return (table_grad, grad_query.reshape(block_rows, feature_width))

    table_grad, grad_queries = lax.scan(
        backward_block,
        jnp.zeros((3 * row_count, 2 * feature_width), jnp.float32),
        (
            query_blocks,
            index_blocks,
            log_totals,
            grad_heads.reshape(block_count, block_rows, feature_width),
        ),
    )
    returned = table_grad[row_count : 2 * row_count]
    for shift_by, side_piece in ((-1, table_grad[:row_count]), (1, table_grad[2 * row_count :])):
        returned = returned + from_behind(
            side_piece.astype(jnp.bfloat16), "patch", shift_by
        ).astype(side_piece.dtype)
    grad_projected = jnp.concatenate(
        [grad_queries.reshape(row_count, feature_width), returned], axis=1
    ).astype(jnp.bfloat16)
    gradient_proj = jnp.einsum(
        "ri,rj->ij", normed, grad_projected, preferred_element_type=jnp.float32
    )
    grad_normed = jnp.einsum("rj,ij->ri", grad_projected, w_qkv, preferred_element_type=jnp.float32)
    grad_input_norm, coeff_attn_grad = norm_back(grad_normed, plain_first, inv_first, coeff_attn)
    grad_input = (grad_residual + grad_input_norm).astype(jnp.bfloat16)
    gradient_proj, gradient_out, gradient_up, gradient_down, coeff_attn_grad, coeff_mlp_grad = (
        lax.psum(
            (
                gradient_proj,
                gradient_out,
                gradient_up,
                gradient_down,
                coeff_attn_grad,
                coeff_mlp_grad,
            ),
            ("patch", "rep"),
        )
    )
    gradient_ada_attn = jnp.outer(cond, coeff_attn_grad)
    gradient_ada_mlp = jnp.outer(cond, coeff_mlp_grad)
    gradient_cond = jnp.dot(ada_attn, coeff_attn_grad, precision=highest) + jnp.dot(
        ada_mlp, coeff_mlp_grad, precision=highest
    )
    leaving = jnp.concatenate([output_rows.astype(jnp.bfloat16), grad_input], axis=1)
    padded = jnp.concatenate([leaving, jnp.zeros((1, 2 * feature_width), jnp.bfloat16)], axis=0)
    going_back = padded[target].reshape(patch_count, capacity, 2 * feature_width)
    home_rows = lax.all_to_all(
        going_back, "patch", split_axis=0, concat_axis=0, tiled=True
    ).reshape(-1, 2 * feature_width)
    band_rows = home_rows[flat_slot]
    return (
        band_rows[:, :feature_width],
        band_rows[:, feature_width:],
        gradient_proj,
        gradient_out,
        gradient_up,
        gradient_down,
        gradient_ada_attn,
        gradient_ada_mlp,
        gradient_cond,
    )


def solution(mesh):
    return jax.shard_map(
        local,
        mesh=mesh,
        in_specs=(
            P(("patch", "rep"), None),
            P(("patch", "rep"), None),
            P(("patch", "rep")),
            P(("patch", "rep"), None),
            P(),
            P(),
            P(),
            P(),
            P(),
            P(),
            P(),
        ),
        out_specs=(
            P(("patch", "rep"), None),
            P(("patch", "rep"), None),
            P(),
            P(),
            P(),
            P(),
            P(),
            P(),
            P(),
        ),
        check_vma=False,
    )
```

profile of v0, /device:TPU:0, one launch (start us, length us, event | category | flops | bytes accessed | tf_op | source)
XLA Modules:
  0.0 489.2 jit_solution(324026931602704912)
XLA Ops:
  10.4 8.3 %all-to-all-start = ((s32[16,1,1]{2,1,0:T(1,128)}), s32[16,1,1]{2,1,0:T(1,128)S(1)}, u32[]{:S(2)}, u32[]{:S(2)}) async-start(s32[16,1,1]{2,1,0:T(1,128)} %copy.43), calls=%async_computation | async-start | bytes 16384 | tf_op jit(solution)/shard_map/all_to_all | solution.py:76
  26.0 5.3 %all-to-all-start.1 = ((bf16[16,17,1024]{2,1,0:T(8,128)(2,1)}), bf16[16,17,1024]{2,1,0:T(8,128)(2,1)S(1)}, u32[]{:S(2)}, u32[]{:S(2)}) async-start(bf16[16,17,1024]{2,1,0:T(8,128)(2,1)} %reshape.284), calls=%async_computation.1 | async-start | bytes 1572864 | tf_op jit(solution)/shard_map/all_to_all | solution.py:69
  32.7 17.8 %all-to-all-done.1 = bf16[16,17,1024]{2,1,0:T(8,128)(2,1)S(1)} async-done(((bf16[16,17,1024]{2,1,0:T(8,128)(2,1)}), bf16[16,17,1024]{2,1,0:T(8,128)(2,1)S(1)}, u32[]{:S(2)}, u32[]{:S(2)}) %all-to-all-start.1) | async-done | bytes 557088 | tf_op jit(solution)/shard_map/all_to_all | solution.py:69
  55.1 5.5 %collective-permute-start.1 = (bf16[256,512]{1,0:T(8,128)(2,1)S(1)}, bf16[256,512]{1,0:T(8,128)(2,1)}, u32[]{:S(2)}, u32[]{:S(2)}) collective-permute-start(bf16[256,512]{1,0:T(8,128)(2,1)S(1)} %fusion.38), channel_id=1, source_target_pairs={{2,0},{4,2},{6,4},{8,6},{10,8},{12,10},{14,12},{16,14},{18,16},{20... | collective-permute-start | bytes 786440 | tf_op jit(solution)/shard_map/ppermute | solution.py:21
  70.6 22.5 %gather_fusion = bf16[4096,1024]{1,0:T(8,128)(2,1)} fusion(bf16[768,1024]{1,0:T(8,128)(2,1)} %pad_maximum_fusion, s32[4096]{0:T(1024)S(1)} %broadcast_clamp_fusion), kind=kCustom, calls=%fused_computation | custom fusion | bytes 16793600 | tf_op jit(solution)/shard_map/while/body/eval_jaxpr/gather | solution.py:120
  93.1 5.9 %slice_bitcast_fusion = (bf16[256,2,4,8,128]{4,3,2,1,0:T(8,128)(2,1)}, bf16[256,2,4,8,128]{4,3,2,1,0:T(8,128)(2,1)S(1)}) fusion(bf16[256,16,1024]{2,1,0:T(8,128)(2,1)} %bitcast.129), kind=kLoop, calls=%fused_computation.22 | loop fusion | bytes 16777216
  105.5 3.5 fusion.7
  116.6 3.6 fusion.93
  126.9 4.4 fusion.9
  131.2 4.9 %multiply_multiply_fusion = f32[256,4,128,16]{2,1,3,0:T(4,128)S(1)} fusion(f32[256,4,16]{1,2,0:T(8,128)S(1)} %copy-done.2, f32[256,4,128]{2,1,0:T(4,128)S(1)} %copy-done.13), kind=kLoop, calls=%fused_computation.13 | loop fusion | flops 4194304 | bytes 8978432 | tf_op jit(solution)/shard_map/while/body/eval_jaxpr/mul | solution.py:205
  136.2 4.2 copy.98
  140.4 2.4 copy.49
  142.8 6.0 %broadcast_multiply_fusion = f32[256,4,128,16]{2,1,3,0:T(4,128)S(1)} fusion(f32[256,4,16]{1,2,0:T(8,128)} %copy.49, f32[256,4,128]{2,1,0:T(4,128)S(1)} %convert.31), kind=kLoop, calls=%fused_computation.24 | loop fusion | flops 2097152 | bytes 8978432 | tf_op jit(solution)/shard_map/while/body/eval_jaxpr/bhj,bhd->bjhd/dot_general | solution.py:208
  148.8 4.2 copy.97
  153.0 37.3 %scatter_custom_fusion.2 = f32[768,1024]{1,0:T(8,128)} fusion(s32[4096]{0:T(1024)} %bitcast.145, f32[4096,512]{1,0:T(8,128)} %bitcast.128, f32[]{:T(128)} %constant.147.clone.1, f32[4096,512]{1,0:T(8,128)} %bitcast.127, f32[]{:T(128)} %constant.132.clone.1), kind=kCustom, calls=%fused_computation.7 | custom fusion | flops 8388608 | bytes 19923968 | tf_op jit(solution)/shard_map/while/body/eval_jaxpr/scatter-add | solution.py:218
  192.5 3.5 collective-permute-start.2
  196.2 2.8 fusion.63
  199.1 8.3 %collective-permute-done.2 = bf16[256,1024]{1,0:T(8,128)(2,1)S(1)} collective-permute-done((bf16[256,1024]{1,0:T(8,128)(2,1)S(1)}, bf16[256,1024]{1,0:T(8,128)(2,1)S(1)}, u32[]{:S(2)}, u32[]{:S(2)}) %collective-permute-start.2) | collective-permute-done | bytes 524320 | tf_op jit(solution)/shard_map/ppermute | solution.py:30
  207.4 9.9 %collective-permute-done.3 = bf16[256,1024]{1,0:T(8,128)(2,1)S(1)} collective-permute-done((bf16[256,1024]{1,0:T(8,128)(2,1)S(1)}, bf16[256,1024]{1,0:T(8,128)(2,1)S(1)}, u32[]{:S(2)}, u32[]{:S(2)}) %collective-permute-start.3) | collective-permute-done | bytes 524320 | tf_op jit(solution)/shard_map/ppermute | solution.py:30
  221.7 3.1 fusion.20
  229.2 5.3 %all-to-all-start.2 = ((bf16[16,17,1024]{2,1,0:T(8,128)(2,1)}), bf16[16,17,1024]{2,1,0:T(8,128)(2,1)S(1)}, u32[]{:S(2)}, u32[]{:S(2)}) async-start(bf16[16,17,1024]{2,1,0:T(8,128)(2,1)} %reshape.294), calls=%async_computation.2 | async-start | bytes 1572864 | tf_op jit(solution)/shard_map/all_to_all | solution.py:266
  234.6 49.8 %all-reduce.1 = (f32[1024]{0:T(1024)S(1)}, f32[1024]{0:T(1024)S(1)}) all-reduce(f32[1024]{0:T(1024)S(1)} %pad_maximum_fusion.4, f32[1024]{0:T(1024)S(1)} %pad_maximum_fusion.5), channel_id=1, replica_groups=mesh['patch'=16,'rep'=2] {'patch','rep'}, use_global_device_ids=true, to_apply=%region_25.26 | all-reduce | flops 2048 | bytes 16384 | tf_op jit(solution)/shard_map/psum | solution.py:246
  288.4 182.0 %all-reduce.5.cloned.1.call-done = (f32[512,1536]{1,0:T(8,128)}, f32[512,512]{1,0:T(8,128)}, f32[512,2048]{1,0:T(8,128)}, f32[2048,512]{1,0:T(8,128)}) async-done(((f32[512,1536]{1,0:T(8,128)}, f32[512,512]{1,0:T(8,128)}, f32[512,2048]{1,0:T(8,128)}, f32[2048,512]{1,0:T(8,128)}), (f32[512,1536]{1,0:T(8,128)}, f32[512,512]{1,0:T(8,128)}, f32[512,2048]{1,0:T(8,128)}, ...) | async-done | bytes 12582928 | tf_op jit(solution)/shard_map/psum | solution.py:246
  470.4 3.9 copy.104
  (200 shorter events, 69.7 us)
Async XLA Ops:
  7.2 103.3 %copy-start = (bf16[512,2048]{1,0:T(8,128)(2,1)S(1)}, bf16[512,2048]{1,0:T(8,128)(2,1)}, u32[]{:S(2)}) copy-start(bf16[512,2048]{1,0:T(8,128)(2,1)} %param.17) | copy-start | bytes 6291460
  7.2 15.7 %copy-start.21 = (f32[32,1024]{1,0:T(8,128)S(1)}, f32[32,1024]{1,0:T(8,128)}, u32[]{:S(2)}) copy-start(f32[32,1024]{1,0:T(8,128)} %param.19) | copy-start | bytes 393220
  7.2 15.7 %copy-start.40 = (f32[32]{0:T(128)S(1)}, f32[32]{0:T(128)}, u32[]{:S(2)}) copy-start(f32[32]{0:T(128)} %param.21) | copy-start | bytes 388
  7.2 15.9 %copy-start.33 = (s32[256,16]{0,1:T(8,128)S(1)}, s32[256,16]{0,1:T(8,128)}, u32[]{:S(2)}) copy-start(s32[256,16]{0,1:T(8,128)} %param.14) | copy-start | bytes 49156
  7.2 16.1 %copy-start.23 = (f32[32,1024]{1,0:T(8,128)S(1)}, f32[32,1024]{1,0:T(8,128)}, u32[]{:S(2)}) copy-start(f32[32,1024]{1,0:T(8,128)} %param.20) | copy-start | bytes 393220
  10.4 15.5 %all-to-all-start = ((s32[16,1,1]{2,1,0:T(1,128)}), s32[16,1,1]{2,1,0:T(1,128)S(1)}, u32[]{:S(2)}, u32[]{:S(2)}) async-start(s32[16,1,1]{2,1,0:T(1,128)} %copy.43), calls=%async_computation | async-start | bytes 16384 | tf_op jit(solution)/shard_map/all_to_all | solution.py:76
  23.1 31.2 %copy-start.29 = (f32[512]{0:T(512)}, f32[512]{0:T(512)S(1)}, u32[]{:S(2)}) copy-start(f32[512]{0:T(512)S(1)} %get-tuple-element.81) | copy-start | bytes 6148
  26.0 24.5 %all-to-all-start.1 = ((bf16[16,17,1024]{2,1,0:T(8,128)(2,1)}), bf16[16,17,1024]{2,1,0:T(8,128)(2,1)S(1)}, u32[]{:S(2)}, u32[]{:S(2)}) async-start(bf16[16,17,1024]{2,1,0:T(8,128)(2,1)} %reshape.284), calls=%async_computation.1 | async-start | bytes 1572864 | tf_op jit(solution)/shard_map/all_to_all | solution.py:69
  31.3 439.1 %all-reduce.5.cloned.1.call-start = ((), (), s32[]{:S(2)}) async-start(), calls=%async_computation.3 | async-start | bytes 25165824 | tf_op jit(solution)/shard_map/psum | solution.py:246
  32.7 21.6 %copy-start.38 = (s32[272]{0:T(512)}, s32[272]{0:T(512)S(1)}, u32[]{:S(2)}) copy-start(s32[272]{0:T(512)S(1)} %fusion.84) | copy-start | bytes 3268
  54.5 10.9 %collective-permute-start = (bf16[256,512]{1,0:T(8,128)(2,1)S(1)}, bf16[256,512]{1,0:T(8,128)(2,1)}, u32[]{:S(2)}, u32[]{:S(2)}) collective-permute-start(bf16[256,512]{1,0:T(8,128)(2,1)S(1)} %fusion.38), channel_id=1, source_target_pairs={{0,2},{2,4},{4,6},{6,8},{8,10},{10,12},{12,14},{14,16},{16,18},{18... | collective-permute-start | bytes 786440 | tf_op jit(solution)/shard_map/ppermute | solution.py:19
  55.1 12.1 %collective-permute-start.1 = (bf16[256,512]{1,0:T(8,128)(2,1)S(1)}, bf16[256,512]{1,0:T(8,128)(2,1)}, u32[]{:S(2)}, u32[]{:S(2)}) collective-permute-start(bf16[256,512]{1,0:T(8,128)(2,1)S(1)} %fusion.38), channel_id=1, source_target_pairs={{2,0},{4,2},{6,4},{8,6},{10,8},{12,10},{14,12},{16,14},{18,16},{20... | collective-permute-start | bytes 786440 | tf_op jit(solution)/shard_map/ppermute | solution.py:21
  93.1 7.9 %copy-start.19 = (bf16[256,4,128,1]{2,3,1,0:T(2,128)(2,1)S(1)}, bf16[256,4,128,1]{2,3,1,0:T(2,128)(2,1)}, u32[]{:S(2)}) copy-start(bf16[256,4,128,1]{2,3,1,0:T(2,128)(2,1)} %reshape.365) | copy-start | bytes 786436
  116.6 5.0 %copy-start.6 = (bf16[256,2,4,8,128]{4,3,2,1,0:T(8,128)(2,1)S(1)}, bf16[256,2,4,8,128]{4,3,2,1,0:T(8,128)(2,1)}, u32[]{:S(2)}) copy-start(bf16[256,2,4,8,128]{4,3,2,1,0:T(8,128)(2,1)} %get-tuple-element.69) | copy-start | bytes 12582916
  190.2 5.8 %copy-start.18 = (f32[256,4,1,128]{3,2,1,0:T(1,128)S(1)}, f32[256,4,1,128]{3,2,1,0:T(1,128)}, u32[]{:S(2)}) copy-start(f32[256,4,1,128]{3,2,1,0:T(1,128)} %fusion.9) | copy-start | bytes 1572868
  192.5 14.9 %collective-permute-start.2 = (bf16[256,1024]{1,0:T(8,128)(2,1)S(1)}, bf16[256,1024]{1,0:T(8,128)(2,1)S(1)}, u32[]{:S(2)}, u32[]{:S(2)}) collective-permute-start(bf16[256,1024]{1,0:T(8,128)(2,1)S(1)} %get-tuple-element.71), channel_id=1, source_target_pairs={{0,30},{2,0},{4,2},{6,4},{8,6},{10,8},{12,10},{14,12},{16,14},{18,... | collective-permute-start | bytes 1572872 | tf_op jit(solution)/shard_map/ppermute | solution.py:30
  196.0 21.2 %collective-permute-start.3 = (bf16[256,1024]{1,0:T(8,128)(2,1)S(1)}, bf16[256,1024]{1,0:T(8,128)(2,1)S(1)}, u32[]{:S(2)}, u32[]{:S(2)}) collective-permute-start(bf16[256,1024]{1,0:T(8,128)(2,1)S(1)} %get-tuple-element.72), channel_id=1, source_target_pairs={{0,2},{2,4},{4,6},{6,8},{8,10},{10,12},{12,14},{14,16},{16,18},{18... | collective-permute-start | bytes 1572872 | tf_op jit(solution)/shard_map/ppermute | solution.py:30
  228.0 6.5 %copy-start.43 = (s32[256]{0:T(256)S(1)}, s32[256]{0:T(256)}, u32[]{:S(2)}) copy-start(s32[256]{0:T(256)} %copy-done.42) | copy-start | bytes 3076
  228.1 6.5 %copy-start.44 = (f32[512]{0:T(512)S(1)}, f32[512]{0:T(512)}, u32[]{:S(2)}) copy-start(f32[512]{0:T(512)} %get-tuple-element.45) | copy-start | bytes 6148
  228.1 6.5 %copy-start.45 = (f32[512]{0:T(512)S(1)}, f32[512]{0:T(512)}, u32[]{:S(2)}) copy-start(f32[512]{0:T(512)} %get-tuple-element.57) | copy-start | bytes 6148
  228.1 56.4 %copy-start.22 = (f32[32,1024]{1,0:T(8,128)S(1)}, f32[32,1024]{1,0:T(8,128)}, u32[]{:S(2)}) copy-start(f32[32,1024]{1,0:T(8,128)} %param.19) | copy-start | bytes 393220
  228.1 56.5 %copy-start.24 = (f32[32,1024]{1,0:T(8,128)S(1)}, f32[32,1024]{1,0:T(8,128)}, u32[]{:S(2)}) copy-start(f32[32,1024]{1,0:T(8,128)} %param.20) | copy-start | bytes 393220
  228.1 57.3 %copy-start.41 = (f32[32]{0:T(128)S(1)}, f32[32]{0:T(128)}, u32[]{:S(2)}) copy-start(f32[32]{0:T(128)} %param.21) | copy-start | bytes 388
  229.2 57.0 %all-to-all-start.2 = ((bf16[16,17,1024]{2,1,0:T(8,128)(2,1)}), bf16[16,17,1024]{2,1,0:T(8,128)(2,1)S(1)}, u32[]{:S(2)}, u32[]{:S(2)}) async-start(bf16[16,17,1024]{2,1,0:T(8,128)(2,1)} %reshape.294), calls=%async_computation.2 | async-start | bytes 1572864 | tf_op jit(solution)/shard_map/all_to_all | solution.py:266
  (32 other events, 87.3 us)
Sparse Core Ops, SparseCore 0:
  221.2 249.1 all-reduce.4
where the time goes:
time: 494 us; the launch traced here: 489 us
  waiting for transfers between devices  221 us (45%)
  local copies, waits for them, and re-layouts  74.2 us (15%)
  other arithmetic  64.3 us (13%)
  blocking collectives  49.8 us (10%)
  matrix products  35.6 us (7%)
  starting transfers between devices  28.7 us (6%)
  between operations  15.1 us (3%)
    psum x1, waiting for transfers between devices, local(): lax.psum((gradient_proj, gradient_out, gradient_up, gradient_down, coeff_...  182 us
    psum x1, blocking collectives, local(): lax.psum((gradient_proj, gradient_out, gradient_up, gradient_down, coeff_...  49.8 us
    scatter-add x1, other arithmetic, backward_block(): table_grad = table_grad.at[index_block.reshape(-1)].add(pair_grad)  37.3 us
    unnamed x102, local copies, waits for them, and re-layouts  31.4 us
    gather x1, local copies, waits for them, and re-layouts, gather_block(): gathered = kv_table[index_block]  22.5 us
    ppermute x2, waiting for transfers between devices, from_behind(): lax.ppermute(array, axis, [(i, (i + by) % size) for i in range(size)])  18.2 us
    all_to_all x1, waiting for transfers between devices, local(): lax.all_to_all(outgoing.reshape(patch_count, capacity, 2 * feature_width)...  17.8 us
  transfers between devices with their start and end apart: 8, of which 6 were waited for; matrix products, arithmetic and copies ran while one was open for 5% of the time, Pallas kernels for 0%

commit v1 on v0

--- a/solution.py
+++ b/solution.py
@@ -244,15 +244,18 @@
     grad_input = (grad_residual + grad_input_norm).astype(jnp.bfloat16)
     gradient_proj, gradient_out, gradient_up, gradient_down, coeff_attn_grad, coeff_mlp_grad = (
         lax.psum(
-            (
-                gradient_proj,
-                gradient_out,
-                gradient_up,
-                gradient_down,
-                coeff_attn_grad,
-                coeff_mlp_grad,
+            lax.psum(
+                (
+                    gradient_proj,
+                    gradient_out,
+                    gradient_up,
+                    gradient_down,
+                    coeff_attn_grad,
+                    coeff_mlp_grad,
+                ),
+                "rep",
             ),
-            ("patch", "rep"),
+            "patch",
         )
     )
     gradient_ada_attn = jnp.outer(cond, coeff_attn_grad)

time: 494 us -> 676 us (1.37)
  waiting for transfers between devices: 221 us -> 394 us
  blocking collectives: 49.8 us -> 62.9 us
    psum x0 -> x1, waiting for transfers between devices: none -> 304 us  [local(): lax.psum(lax.psum((gradient_proj, gradient_out, gradient_up, gradient_dow...]
    psum x1, waiting for transfers between devices: 182 us -> 49.2 us  [local(): lax.psum((gradient_proj, gradient_out, gradient_up, gradient_down, coeff_...]
    psum x0 -> x1, blocking collectives: none -> 60.4 us  [local(): lax.psum(lax.psum((gradient_proj, gradient_out, gradient_up, gradient_dow...]
    psum x1, blocking collectives: 49.8 us -> 2.5 us  [local(): lax.psum((gradient_proj, gradient_out, gradient_up, gradient_down, coeff_...]
  transfers between devices with their start and end apart: 8 -> 9, of which waited for: 6 -> 7; matrix products, arithmetic and copies ran while one was open for 5% -> 4% of each run, Pallas kernels for 0% -> 0%
where the time goes in v1:
time: 676 us; the launch traced here: 675 us
  waiting for transfers between devices  394 us (58%)
  local copies, waits for them, and re-layouts  74.1 us (11%)
  other arithmetic  64.3 us (10%)
  blocking collectives  62.9 us (9%)
  matrix products  35.6 us (5%)
  starting transfers between devices  29.3 us (4%)
  between operations  14.9 us (2%)
    psum x1, waiting for transfers between devices, local(): lax.psum(lax.psum((gradient_proj, gradient_out, gradient_up, gradient_dow...  304 us
    psum x1, blocking collectives, local(): lax.psum(lax.psum((gradient_proj, gradient_out, gradient_up, gradient_dow...  60.4 us
    psum x1, waiting for transfers between devices, local(): lax.psum((gradient_proj, gradient_out, gradient_up, gradient_down, coeff_...  49.2 us
    scatter-add x1, other arithmetic, backward_block(): table_grad = table_grad.at[index_block.reshape(-1)].add(pair_grad)  37.3 us
    unnamed x102, local copies, waits for them, and re-layouts  31.5 us
    gather x1, local copies, waits for them, and re-layouts, gather_block(): gathered = kv_table[index_block]  22.5 us
    ppermute x2, waiting for transfers between devices, from_behind(): lax.ppermute(array, axis, [(i, (i + by) % size) for i in range(size)])  18.8 us
    all_to_all x1, waiting for transfers between devices, local(): lax.all_to_all(outgoing.reshape(patch_count, capacity, 2 * feature_width)...  17.8 us
  transfers between devices with their start and end apart: 9, of which 7 were waited for; matrix products, arithmetic and copies ran while one was open for 4% of the time, Pallas kernels for 0%

profile of v1, /device:TPU:0, one launch (start us, length us, event | category | flops | bytes accessed | tf_op | source)
XLA Modules:
  0.0 675.1 jit_solution(11039892625412253030)
XLA Ops:
  10.4 8.3 %all-to-all-start = ((s32[16,1,1]{2,1,0:T(1,128)}), s32[16,1,1]{2,1,0:T(1,128)S(1)}, u32[]{:S(2)}, u32[]{:S(2)}) async-start(s32[16,1,1]{2,1,0:T(1,128)} %copy.43), calls=%async_computation | async-start | bytes 16384 | tf_op jit(solution)/shard_map/all_to_all | solution.py:76
  26.0 5.3 all-to-all-start.1
  32.7 17.8 %all-to-all-done.1 = bf16[16,17,1024]{2,1,0:T(8,128)(2,1)S(1)} async-done(((bf16[16,17,1024]{2,1,0:T(8,128)(2,1)}), bf16[16,17,1024]{2,1,0:T(8,128)(2,1)S(1)}, u32[]{:S(2)}, u32[]{:S(2)}) %all-to-all-start.1) | async-done | bytes 557088 | tf_op jit(solution)/shard_map/all_to_all | solution.py:69
  55.1 5.1 collective-permute-start.1
  70.6 22.5 %gather_fusion = bf16[4096,1024]{1,0:T(8,128)(2,1)} fusion(bf16[768,1024]{1,0:T(8,128)(2,1)} %pad_maximum_fusion, s32[4096]{0:T(1024)S(1)} %broadcast_clamp_fusion), kind=kCustom, calls=%fused_computation | custom fusion | bytes 16793600 | tf_op jit(solution)/shard_map/while/body/eval_jaxpr/gather | solution.py:120
  93.1 5.9 slice_bitcast_fusion
  105.5 3.5 fusion.7
  116.5 3.6 fusion.93
  126.8 4.4 fusion.9
  131.2 4.9 multiply_multiply_fusion
  136.1 4.2 copy.98
  142.7 6.0 broadcast_multiply_fusion
  148.7 4.2 copy.97
  152.9 37.3 %scatter_custom_fusion.2 = f32[768,1024]{1,0:T(8,128)} fusion(s32[4096]{0:T(1024)} %bitcast.145, f32[4096,512]{1,0:T(8,128)} %bitcast.128, f32[]{:T(128)} %constant.147.clone.1, f32[4096,512]{1,0:T(8,128)} %bitcast.127, f32[]{:T(128)} %constant.132.clone.1), kind=kCustom, calls=%fused_computation.7 | custom fusion | flops 8388608 | bytes 19923968 | tf_op jit(solution)/shard_map/while/body/eval_jaxpr/scatter-add | solution.py:218
  192.5 3.1 collective-permute-start.2
  195.8 2.8 fusion.63
  198.6 8.8 %collective-permute-done.2 = bf16[256,1024]{1,0:T(8,128)(2,1)S(1)} collective-permute-done((bf16[256,1024]{1,0:T(8,128)(2,1)S(1)}, bf16[256,1024]{1,0:T(8,128)(2,1)S(1)}, u32[]{:S(2)}, u32[]{:S(2)}) %collective-permute-start.2) | collective-permute-done | bytes 524320 | tf_op jit(solution)/shard_map/ppermute | solution.py:30
  207.4 10.0 %collective-permute-done.3 = bf16[256,1024]{1,0:T(8,128)(2,1)S(1)} collective-permute-done((bf16[256,1024]{1,0:T(8,128)(2,1)S(1)}, bf16[256,1024]{1,0:T(8,128)(2,1)S(1)}, u32[]{:S(2)}, u32[]{:S(2)}) %collective-permute-start.3) | collective-permute-done | bytes 524320 | tf_op jit(solution)/shard_map/ppermute | solution.py:30
  221.2 49.2 %all-reduce.10.cloned.1.call-done = (f32[512,1536]{1,0:T(8,128)}, f32[512,512]{1,0:T(8,128)}, f32[512,2048]{1,0:T(8,128)}, f32[2048,512]{1,0:T(8,128)}) async-done(((f32[512,1536]{1,0:T(8,128)}, f32[512,512]{1,0:T(8,128)}, f32[512,2048]{1,0:T(8,128)}, f32[2048,512]{1,0:T(8,128)}), (f32[512,1536]{1,0:T(8,128)}, f32[512,512]{1,0:T(8,128)}, f32[512,2048]{1,0:T(8,128)}, ...) | async-done | bytes 12582928 | tf_op jit(solution)/shard_map/psum | solution.py:247
  271.1 3.1 fusion.20
  278.6 6.8 %all-to-all-start.2 = ((bf16[16,17,1024]{2,1,0:T(8,128)(2,1)}), bf16[16,17,1024]{2,1,0:T(8,128)(2,1)S(1)}, u32[]{:S(2)}, u32[]{:S(2)}) async-start(bf16[16,17,1024]{2,1,0:T(8,128)(2,1)} %reshape.294), calls=%async_computation.2 | async-start | bytes 1572864 | tf_op jit(solution)/shard_map/all_to_all | solution.py:269
  287.9 60.4 %all-reduce.1 = (f32[1024]{0:T(1024)S(1)}, f32[1024]{0:T(1024)S(1)}) all-reduce(f32[1024]{0:T(1024)S(1)} %get-tuple-element.67, f32[1024]{0:T(1024)S(1)} %get-tuple-element.68), channel_id=1, replica_groups=mesh['patch'=16,'rep'=2] {'patch'}, use_global_device_ids=true, to_apply=%region_30.31 | all-reduce | flops 2048 | bytes 16384 | tf_op jit(solution)/shard_map/psum | solution.py:246
  352.3 304.3 %all-reduce.8.cloned.1.call-done = (f32[512,1536]{1,0:T(8,128)}, f32[512,512]{1,0:T(8,128)}, f32[512,2048]{1,0:T(8,128)}, f32[2048,512]{1,0:T(8,128)}) async-done(((f32[512,1536]{1,0:T(8,128)}, f32[512,512]{1,0:T(8,128)}, f32[512,2048]{1,0:T(8,128)}, f32[2048,512]{1,0:T(8,128)}), (f32[512,1536]{1,0:T(8,128)}, f32[512,512]{1,0:T(8,128)}, f32[512,2048]{1,0:T(8,128)}, ...) | async-done | bytes 12582928 | tf_op jit(solution)/shard_map/psum | solution.py:246
  656.6 3.9 copy.108
  (204 shorter events, 75.0 us)
Async XLA Ops:
  7.2 103.3 %copy-start = (bf16[512,2048]{1,0:T(8,128)(2,1)S(1)}, bf16[512,2048]{1,0:T(8,128)(2,1)}, u32[]{:S(2)}) copy-start(bf16[512,2048]{1,0:T(8,128)(2,1)} %param.17) | copy-start | bytes 6291460
  7.2 15.7 %copy-start.21 = (f32[32,1024]{1,0:T(8,128)S(1)}, f32[32,1024]{1,0:T(8,128)}, u32[]{:S(2)}) copy-start(f32[32,1024]{1,0:T(8,128)} %param.19) | copy-start | bytes 393220
  7.2 15.7 %copy-start.40 = (f32[32]{0:T(128)S(1)}, f32[32]{0:T(128)}, u32[]{:S(2)}) copy-start(f32[32]{0:T(128)} %param.21) | copy-start | bytes 388
  7.2 15.9 %copy-start.33 = (s32[256,16]{0,1:T(8,128)S(1)}, s32[256,16]{0,1:T(8,128)}, u32[]{:S(2)}) copy-start(s32[256,16]{0,1:T(8,128)} %param.14) | copy-start | bytes 49156
  7.2 16.1 %copy-start.23 = (f32[32,1024]{1,0:T(8,128)S(1)}, f32[32,1024]{1,0:T(8,128)}, u32[]{:S(2)}) copy-start(f32[32,1024]{1,0:T(8,128)} %param.20) | copy-start | bytes 393220
  10.4 15.5 %all-to-all-start = ((s32[16,1,1]{2,1,0:T(1,128)}), s32[16,1,1]{2,1,0:T(1,128)S(1)}, u32[]{:S(2)}, u32[]{:S(2)}) async-start(s32[16,1,1]{2,1,0:T(1,128)} %copy.43), calls=%async_computation | async-start | bytes 16384 | tf_op jit(solution)/shard_map/all_to_all | solution.py:76
  23.1 31.2 %copy-start.29 = (f32[512]{0:T(512)}, f32[512]{0:T(512)S(1)}, u32[]{:S(2)}) copy-start(f32[512]{0:T(512)S(1)} %get-tuple-element.87) | copy-start | bytes 6148
  26.0 24.5 %all-to-all-start.1 = ((bf16[16,17,1024]{2,1,0:T(8,128)(2,1)}), bf16[16,17,1024]{2,1,0:T(8,128)(2,1)S(1)}, u32[]{:S(2)}, u32[]{:S(2)}) async-start(bf16[16,17,1024]{2,1,0:T(8,128)(2,1)} %reshape.284), calls=%async_computation.1 | async-start | bytes 1572864 | tf_op jit(solution)/shard_map/all_to_all | solution.py:69
  31.3 239.1 %all-reduce.10.cloned.1.call-start = ((), (), s32[]{:S(2)}) async-start(), calls=%async_computation.4 | async-start | bytes 25165824 | tf_op jit(solution)/shard_map/psum | solution.py:247
  32.7 21.6 %copy-start.38 = (s32[272]{0:T(512)}, s32[272]{0:T(512)S(1)}, u32[]{:S(2)}) copy-start(s32[272]{0:T(512)S(1)} %fusion.84) | copy-start | bytes 3268
  54.5 10.4 %collective-permute-start = (bf16[256,512]{1,0:T(8,128)(2,1)S(1)}, bf16[256,512]{1,0:T(8,128)(2,1)}, u32[]{:S(2)}, u32[]{:S(2)}) collective-permute-start(bf16[256,512]{1,0:T(8,128)(2,1)S(1)} %fusion.38), channel_id=1, source_target_pairs={{0,2},{2,4},{4,6},{6,8},{8,10},{10,12},{12,14},{14,16},{16,18},{18... | collective-permute-start | bytes 786440 | tf_op jit(solution)/shard_map/ppermute | solution.py:19
  55.1 12.1 %collective-permute-start.1 = (bf16[256,512]{1,0:T(8,128)(2,1)S(1)}, bf16[256,512]{1,0:T(8,128)(2,1)}, u32[]{:S(2)}, u32[]{:S(2)}) collective-permute-start(bf16[256,512]{1,0:T(8,128)(2,1)S(1)} %fusion.38), channel_id=1, source_target_pairs={{2,0},{4,2},{6,4},{8,6},{10,8},{12,10},{14,12},{16,14},{18,16},{20... | collective-permute-start | bytes 786440 | tf_op jit(solution)/shard_map/ppermute | solution.py:21
  93.1 7.9 %copy-start.19 = (bf16[256,4,128,1]{2,3,1,0:T(2,128)(2,1)S(1)}, bf16[256,4,128,1]{2,3,1,0:T(2,128)(2,1)}, u32[]{:S(2)}) copy-start(bf16[256,4,128,1]{2,3,1,0:T(2,128)(2,1)} %reshape.365) | copy-start | bytes 786436
  190.2 5.4 copy-start.18
  192.5 14.9 %collective-permute-start.2 = (bf16[256,1024]{1,0:T(8,128)(2,1)S(1)}, bf16[256,1024]{1,0:T(8,128)(2,1)S(1)}, u32[]{:S(2)}, u32[]{:S(2)}) collective-permute-start(bf16[256,1024]{1,0:T(8,128)(2,1)S(1)} %get-tuple-element.77), channel_id=1, source_target_pairs={{0,30},{2,0},{4,2},{6,4},{8,6},{10,8},{12,10},{14,12},{16,14},{18,... | collective-permute-start | bytes 1572872 | tf_op jit(solution)/shard_map/ppermute | solution.py:30
  195.6 21.8 %collective-permute-start.3 = (bf16[256,1024]{1,0:T(8,128)(2,1)S(1)}, bf16[256,1024]{1,0:T(8,128)(2,1)S(1)}, u32[]{:S(2)}, u32[]{:S(2)}) collective-permute-start(bf16[256,1024]{1,0:T(8,128)(2,1)S(1)} %get-tuple-element.78), channel_id=1, source_target_pairs={{0,2},{2,4},{4,6},{6,8},{8,10},{10,12},{12,14},{14,16},{16,18},{18... | collective-permute-start | bytes 1572872 | tf_op jit(solution)/shard_map/ppermute | solution.py:30
  221.2 435.4 %all-reduce.8.cloned.1.call-start = ((), (), s32[]{:S(2)}) async-start(), calls=%async_computation.3 | async-start | bytes 25165824 | tf_op jit(solution)/shard_map/psum | solution.py:246
  277.4 7.9 %copy-start.43 = (s32[256]{0:T(256)S(1)}, s32[256]{0:T(256)}, u32[]{:S(2)}) copy-start(s32[256]{0:T(256)} %copy-done.42) | copy-start | bytes 3076
  277.4 8.0 %copy-start.44 = (f32[512]{0:T(512)S(1)}, f32[512]{0:T(512)}, u32[]{:S(2)}) copy-start(f32[512]{0:T(512)} %get-tuple-element.45) | copy-start | bytes 6148
  277.4 8.0 %copy-start.45 = (f32[512]{0:T(512)S(1)}, f32[512]{0:T(512)}, u32[]{:S(2)}) copy-start(f32[512]{0:T(512)} %get-tuple-element.57) | copy-start | bytes 6148
  277.4 70.9 %copy-start.22 = (f32[32,1024]{1,0:T(8,128)S(1)}, f32[32,1024]{1,0:T(8,128)}, u32[]{:S(2)}) copy-start(f32[32,1024]{1,0:T(8,128)} %param.19) | copy-start | bytes 393220
  277.5 71.1 %copy-start.24 = (f32[32,1024]{1,0:T(8,128)S(1)}, f32[32,1024]{1,0:T(8,128)}, u32[]{:S(2)}) copy-start(f32[32,1024]{1,0:T(8,128)} %param.20) | copy-start | bytes 393220
  277.5 71.9 %copy-start.41 = (f32[32]{0:T(128)S(1)}, f32[32]{0:T(128)}, u32[]{:S(2)}) copy-start(f32[32]{0:T(128)} %param.21) | copy-start | bytes 388
  278.6 71.5 %all-to-all-start.2 = ((bf16[16,17,1024]{2,1,0:T(8,128)(2,1)}), bf16[16,17,1024]{2,1,0:T(8,128)(2,1)S(1)}, u32[]{:S(2)}, u32[]{:S(2)}) async-start(bf16[16,17,1024]{2,1,0:T(8,128)(2,1)} %reshape.294), calls=%async_computation.2 | async-start | bytes 1572864 | tf_op jit(solution)/shard_map/all_to_all | solution.py:269
  (33 other events, 92.4 us)
Sparse Core Ops, SparseCore 0:
  221.3 49.0 all-reduce.9
  276.8 379.7 all-reduce.7
